TPU v7x, 256 devices: a whole 4x4x8 slice. The times are simulated.
256 devices in a mesh: space: 8 (over y, core), dev: 32 (over x, z).
Axes of the slice: x: 4, y: 4, z: 8, core: 2. Of those that a mesh axis runs over, the one named last changes fastest.
Arguments:
- density_matrix: float32 [4096, 4096], P(('space', 'dev')), may hold values from -0.2 to 0.2
- basis: float32 [512, 384, 1024], P(('space', 'dev')), may hold values from -1.6 to 1.6
- union: int32 [512, 8], P(('space', 'dev')), may hold values from 0 to 31, as said below
- weights: float32 [512, 384], P(('space', 'dev')), may hold values from 0.2 to 2
- in_scale: float32 [256], replicated, may hold values from 0.3 to 3
- in_shift: float32 [256], replicated, may hold values from -1 to 1
- hidden_weight: float32 [256, 256], replicated, may hold values from -0.375 to 0.375
- hidden_bias: float32 [256], replicated, may hold values from -3 to 3
- out_weight: float32 [256], replicated, may hold values from -0.375 to 0.375
Outputs:
- density: float32 [512, 384], P(('space', 'dev'))
- potential: float32 [4096, 4096], P(('space', 'dev'))
Inputs may be any that keep to these rules, and one draw needn't show every extreme that they name: `union`: row b lists 8 distinct tiles, all among tiles (g - 1) * 4 to (g + 2) * 4 - 1, where g = b // 64.
All inputs are finite; a program needn't handle non-finite values.
Results may differ from a plain program's by a relative error of at most 0.00011.
Values sent between devices are 32-bit elements; how exact they have to be, the bound alone decides.
A program may use at most 128 MiB of HBM per device.

v0:
```python
import functools
import heapq

import jax
import jax.numpy as jnp
from jax import lax
from jax.experimental import pallas as pl
from jax.experimental.pallas import tpu as pltpu
from jax.sharding import PartitionSpec as P

MESH = pl.DeviceIdType.MESH
TILE = 128
U = 8
NX, NZ = 4, 8
NS = 8
ROWS = 16
WT = 12
ND = 7
STRIPS = 3 * ND
PB = 384
NP = 2 * PB
NPAIR = WT // 2
SPAN = 8 * TILE
WIDE = (WT + 6) * TILE
GRID_TILES = 32

CLASSES = (
    (0, 6, True, 1),
    (6, 12, True, -1),
    (12, 17, False, 1),
    (17, 21, False, -1),
)


def class_nodes(sign):
    xs = (0, 1, -1, 2 * sign)
    zs = (0, 1, -1, 2, -2, 3, -3, 4 * sign)
    return [(dx, dz) for dx in xs for dz in zs if (dx, dz) != (0, 0)]


def parent_of(node, z_first):
    dx, dz = node
    step_x = (dx > 0) - (dx < 0)
    step_z = (dz > 0) - (dz < 0)
    if z_first:
        return ((dx - step_x, dz), (step_x, 0)) if dx else ((0, dz - step_z), (0, step_z))
    return ((dx, dz - step_z), (0, step_z)) if dz else ((dx - step_x, 0), (step_x, 0))


def plan():
    children = {}
    for c, (lo, hi, z_first, sign) in enumerate(CLASSES):
        for node in class_nodes(sign):
            par, step = parent_of(node, z_first)
            children.setdefault((c, par), []).append((c, node, step))
    latency = 14.0
    free = {}
    heap = []
    order = []

    def push(now, kids):
        for c, node, step in kids:
            lo, hi = CLASSES[c][:2]
            start = max(now, free.get(step, 0.0))
            free[step] = start + (hi - lo)
            heapq.heappush(heap, (free[step] + latency, c, node, step))

    first, later = [], []
    for c, (lo, hi, z_first, sign) in enumerate(CLASSES):
        for kid in children[(c, (0, 0))]:
            lead = (kid[2][1] != 0) == z_first
            (first if lead else later).append(kid)
    roots = first + later
    push(0.0, roots)
    while heap:
        now, c, node, step = heapq.heappop(heap)
        order.append((c, node, step))
        push(now, children.get((c, node), []))
    return roots, order, children


ROOTS, ORDER, CHILDREN = plan()
NODE_ID = {}
for _c in range(len(CLASSES)):
    for _k, _node in enumerate(class_nodes(CLASSES[_c][3])):
        NODE_ID[(_c, _node)] = _k
NN = NX * NZ - 1


def split(value):
    high = value.astype(jnp.bfloat16)
    low = (value - high.astype(jnp.float32)).astype(jnp.bfloat16)
    return high, low


def swap_groups(parts):
    lane = lax.broadcasted_iota(jnp.int32, (ROWS, TILE), 1) // ROWS
    parts = list(parts)
    for bit in range(3):
        d = 1 << bit
        upper = (lane // d) % 2 == 1
        for i in range(8):
            if i & d:
                continue
            a, b = parts[i], parts[i + d]
            parts[i] = jnp.where(upper, pltpu.roll(b, ROWS * d, 1), a)
            parts[i + d] = jnp.where(upper, b, pltpu.roll(a, TILE - ROWS * d, 1))
    return parts


def fdot(a, b):
    return jnp.dot(a, b, preferred_element_type=jnp.float32)


def kernel(
    union_ref, rows_ref, basis_hbm, weights_ref, scale_ref, shift_ref, hidden_ref, bias_ref, out_w_ref,
    density_ref, potential_ref,
    basis_ref, full_ref, v3_ref, bth_ref, btl_ref, sh_ref, sl_ref, t3_ref,
    gath_ref, part_ref, land_ref,
    mine_ref, msend_ref, mrecv_ref, tt_ref, dsend_ref, dland_ref, tland_ref,
    mrecv2_ref, msend2_ref, ss_ref, dland2_ref, tland2_ref,
    basis_sem, ag_send, ag_recv, rs_send, rs_recv,
    m_send, m_recv, d_send, d_recv, t_send, t_recv,
    m2_send, m2_recv, d2_send, d2_recv, t2_send, t2_recv,
):
    region = lax.axis_index("space")
    dev = lax.axis_index("dev")
    x = dev // NZ
    z = dev % NZ

    def device(dr, dx, dz):
        return {
            "space": (region + dr + NS) % NS,
            "dev": ((x + dx + 2 * NX) % NX) * NZ + (z + dz + NZ) % NZ,
        }

    load = pltpu.make_async_copy(basis_hbm, basis_ref, basis_sem)
    load.start()

    barrier = pltpu.get_barrier_semaphore()
    peers = [(0, 0, dz) for dz in range(1, NZ)]
    peers += [(dr, dx, 0) for dr in (-1, 0, 1) for dx in range(NX) if (dr, dx) != (0, 0)]
    for peer in peers:
        pl.semaphore_signal(barrier, inc=1, device_id=device(*peer), device_id_type=MESH)

    sent = []

    def remote(src, dst, send_sem, recv_sem, where):
        return pltpu.make_async_remote_copy(
            src_ref=src, dst_ref=dst, send_sem=send_sem, recv_sem=recv_sem,
            device_id=device(*where), device_id_type=MESH,
        )

    def go(*args):
        copy = remote(*args)
        copy.start()
        sent.append(copy)

    def row_tile(tile):
        tile = (tile + 2 * GRID_TILES) % GRID_TILES
        return pl.ds(pl.multiple_of(tile * TILE, TILE), TILE)

    my_tile = region * 4 + x

    for dr in (-1, 0, 1):
        i = x + 4 * (1 - dr)
        base = 4 * (region + dr - 1)
        for delta in range(ND):
            strip = rows_ref[:, row_tile(base + (i + delta) % WT)]
            if dr == 0:
                mine_ref[ND + delta] = strip
            else:
                dsend_ref[(dr + 1) // 2, delta] = strip
    slots = []
    for delta in range(1, 6):
        for wrap in range(2):
            slots.append(rows_ref[:, row_tile(my_tile - delta + WT * wrap)])
    zero = jnp.zeros((ROWS, TILE), jnp.float32)
    slots += [zero] * (16 - len(slots))
    for grp in range(2):
        for zz, part in enumerate(swap_groups(slots[8 * grp : 8 * grp + 8])):
            msend_ref[zz, grp] = part

    pl.semaphore_wait(barrier, len(peers))
    for k in range(1, NZ):
        go(msend_ref.at[(z + k) % NZ], mrecv_ref.at[z], m_send.at[k - 1], m_recv.at[k - 1], (0, 0, k))
    for k, dr in enumerate((-1, 1)):
        go(dsend_ref.at[k], dland_ref.at[k], d_send.at[k], d_recv.at[k], (dr, 0, 0))
    mrecv_ref[z] = msend_ref[z]

    for k in range(1, NZ):
        slot = mrecv_ref.at[(z - k + NZ) % NZ]
        remote(slot, slot, m_send.at[k - 1], m_recv.at[k - 1], (0, 0, k)).wait_recv()
    for grp in range(2):
        stacked = mrecv_ref[:, grp].reshape(TILE, TILE).T
        for e in range(8):
            if 8 * grp + e < 10:
                tt_ref[8 * grp + e] = stacked[ROWS * e : ROWS * (e + 1)]

    kinds = [(k, dr, delta) for k, (dr, delta) in enumerate((r, d) for r in (-1, 0, 1) for d in range(1, 6))]
    for k, dr, delta in kinds:
        j = x + 4 * (1 - dr)
        wrap = 1 - (j - delta + WT) // WT
        e = 2 * (delta - 1) + wrap
        if dr == 0 and delta == 4:
            tland_ref[k] = tt_ref[e]
        else:
            go(tt_ref.at[e], tland_ref.at[k], t_send.at[k], t_recv.at[k], (dr, -delta, 0))

    for k, dr in enumerate((-1, 1)):
        slot = dland_ref.at[k]
        remote(slot, slot, d_send.at[k], d_recv.at[k], (dr, 0, 0)).wait_recv()
        first = ND * (1 - dr)
        mine_ref[pl.ds(first, ND)] = dland_ref[k]
    for k, dr, delta in kinds:
        if not (dr == 0 and delta == 4):
            slot = tland_ref.at[k]
            remote(slot, slot, t_send.at[k], t_recv.at[k], (dr, -delta, 0)).wait_recv()
        j = (x + delta) % NX + 4 * (1 - dr)
        i = (j - delta + WT) % WT
        s = (i // 4) * ND + delta
        mine_ref[s] += tland_ref[k]
    gath_ref[x, z] = mine_ref[...]

    def block(ref, dx, dz, lo, hi):
        return ref.at[(x - dx + 2 * NX) % NX, (z - dz + NZ) % NZ, lo:hi]

    def forward(c, node, step, at):
        lo, hi = CLASSES[c][:2]
        k = c * NN + NODE_ID[(c, node)]
        view = block(gath_ref, at[0], at[1], lo, hi)
        go(view, view, ag_send.at[k], ag_recv.at[k], (0, step[0], step[1]))

    for c, node, step in ROOTS:
        forward(c, node, step, (0, 0))

    first_tile = 4 * (region - 1)

    def prepare(t, carry):
        for b in range(2):
            value = None
            for s in range(U):
                hit = (union_ref[b, s] == first_tile + t).astype(jnp.float32)
                term = basis_ref[b, :, s * TILE : (s + 1) * TILE] * hit
                value = term if value is None else value + term
            high, low = split(value)
            rows = pl.ds(b * PB, PB)
            full_ref[rows, pl.ds(pl.multiple_of(t * TILE, TILE), TILE)] = value

            @pl.when(t < 6)
            def _():
                full_ref[rows, pl.ds(pl.multiple_of((t + WT) * TILE, TILE), TILE)] = value

            p = t // 2
            off = (t % 2) * TILE
            for part, src in enumerate((high, low, high)):
                v3_ref[p, rows, pl.ds(pl.multiple_of(off + 256 * part, TILE), TILE)] = src
            high_t, low_t = split(value.T)
            tile_rows = pl.ds(pl.multiple_of(t * TILE, TILE), TILE)
            bth_ref[tile_rows, b * PB : (b + 1) * PB] = high_t
            btl_ref[tile_rows, b * PB : (b + 1) * PB] = low_t
        return carry

    t3_ref[...] = jnp.zeros_like(t3_ref)
    pieces = {6: (0, 2), 18: (2, 4), 30: (4, 6), 42: (6, 8), 54: (8, 10), 66: (10, 12)}
    load.wait()
    for n, (c, node, step) in enumerate(ORDER):
        lo, hi = CLASSES[c][:2]
        k = c * NN + NODE_ID[(c, node)]
        view = block(gath_ref, node[0], node[1], lo, hi)
        remote(view, view, ag_send.at[k], ag_recv.at[k], (0, step[0], step[1])).wait_recv()
        for kid in CHILDREN.get((c, node), []):
            forward(*kid, node)
        if n in pieces:
            lax.fori_loop(*pieces[n], prepare, 0)

    def pair_density(p, acc):
        for h in range(2):
            i = 2 * p + h
            for delta in range(ND):
                tile = gath_ref[i % 4, :, (i // 4) * ND + delta].reshape(TILE, TILE)
                high, low = split(tile)
                cols = slice((h + delta) * TILE, (h + delta + 1) * TILE)
                t3_ref[TILE * h : TILE * (h + 1), cols] = high
                t3_ref[256 + TILE * h : 256 + TILE * (h + 1), cols] = high
                t3_ref[512 + TILE * h : 512 + TILE * (h + 1), cols] = low
        for q in range(4):
            res = fdot(v3_ref[p], t3_ref[:, 256 * q : 256 * (q + 1)])
            other = full_ref[:, pl.ds(pl.multiple_of(p * 256 + 256 * q, TILE), 256)]
            res = res * other
            acc = acc + res[:, :TILE] + res[:, TILE:]
        return acc

    acc = lax.fori_loop(0, NPAIR, pair_density, jnp.zeros((NP, TILE), jnp.float32))
    rho = jnp.sum(acc, axis=1, keepdims=True)

    hid_high, hid_low = split(hidden_ref[...])
    first = jnp.tanh(rho * scale_ref[...] + shift_ref[...])
    high, low = split(first)
    pre = fdot(high, hid_high) + fdot(low, hid_high) + fdot(high, hid_low) + bias_ref[...]
    second = pre / (1.0 + jnp.exp(-pre))
    pot = jnp.sum(second * out_w_ref[...], axis=1, keepdims=True)
    for b in range(2):
        rho_b = jnp.broadcast_to(rho[b * PB : (b + 1) * PB], (PB, TILE)).T
        density_ref[b : b + 1, :] = rho_b[0:1]
        w_b = jnp.broadcast_to(weights_ref[b : b + 1, :], (TILE, PB)).T
        factor = w_b[:, 0:1] * pot[b * PB : (b + 1) * PB]

        def scale_tile(t, carry):
            cols = pl.ds(pl.multiple_of(t * TILE, TILE), TILE)
            rows = pl.ds(b * PB, PB)
            high, low = split(full_ref[rows, cols] * factor)
            sh_ref[rows, cols] = high
            sl_ref[rows, cols] = low
            return carry

        lax.fori_loop(0, WIDE // TILE, scale_tile, 0)

    def pair_part(p, carry):
        rows = pl.ds(pl.multiple_of(p * 256, 256), 256)
        left_high, left_low = bth_ref[rows], btl_ref[rows]
        for q in range(4):
            cols = pl.ds(pl.multiple_of(p * 256 + 256 * q, TILE), 256)
            right_high = sh_ref[:, cols]
            res = fdot(left_high, right_high) + fdot(left_low, right_high) + fdot(left_high, sl_ref[:, cols])
            for h in range(2):
                i = 2 * p + h
                for w in range(2):
                    delta = 2 * q + w - h
                    if 0 <= delta < ND:
                        piece = res[h * TILE : (h + 1) * TILE, w * TILE : (w + 1) * TILE]
                        part_ref[i % 4, :, (i // 4) * ND + delta] = piece.reshape(NZ, ROWS, TILE)
        return carry

    lax.fori_loop(0, NPAIR, pair_part, 0)

    def add_children(c, node):
        lo, hi = CLASSES[c][:2]
        bx, bz = (x - node[0] + 2 * NX) % NX, (z - node[1] + NZ) % NZ
        for _, kid, step in CHILDREN.get((c, node), []):
            k = NODE_ID[(c, kid)]
            slot = land_ref.at[k, lo:hi]
            sem = c * NN + k
            remote(slot, slot, rs_send.at[sem], rs_recv.at[sem], (0, -step[0], -step[1])).wait_recv()
            part_ref[bx, bz, lo:hi] += land_ref[k, lo:hi]

    for c, node, step in reversed(ORDER):
        add_children(c, node)
        lo, hi = CLASSES[c][:2]
        k = NODE_ID[(c, node)]
        go(
            block(part_ref, node[0], node[1], lo, hi), land_ref.at[k, lo:hi],
            rs_send.at[c * NN + k], rs_recv.at[c * NN + k], (0, -step[0], -step[1]),
        )
    for c in reversed(range(len(CLASSES))):
        add_children(c, (0, 0))

    own = part_ref.at[x, z]
    for k, dr in enumerate((-1, 1)):
        go(own.at[pl.ds(ND * (1 + dr), ND)], dland2_ref.at[k], d2_send.at[k], d2_recv.at[k], (dr, 0, 0))
    ss_ref[...] = jnp.zeros_like(ss_ref)

    def transposed_slot(xx, dr, delta):
        j = xx + 4 * (1 - dr)
        wrap = 1 - (j - delta + WT) // WT
        return 2 * (delta - 1) + wrap

    for k, dr, delta in kinds:
        j = (x + delta) % NX + 4 * (1 - dr)
        i = (j - delta + WT) % WT
        s = (i // 4) * ND + delta
        if dr == 0 and delta == 4:
            ss_ref[transposed_slot(x, dr, delta)] += part_ref[x, z, s]
        else:
            go(own.at[s], tland2_ref.at[k], t2_send.at[k], t2_recv.at[k], (-dr, delta, 0))
    for k, dr, delta in kinds:
        if dr == 0 and delta == 4:
            continue
        slot = tland2_ref.at[k]
        remote(slot, slot, t2_send.at[k], t2_recv.at[k], (-dr, delta, 0)).wait_recv()
        ss_ref[transposed_slot(x, dr, delta)] += tland2_ref[k]
    for grp in range(2):
        stacked = ss_ref[8 * grp : 8 * grp + 8].reshape(TILE, TILE).T
        for zz in range(NZ):
            msend2_ref[zz, grp] = stacked[ROWS * zz : ROWS * (zz + 1)]
    for k in range(1, NZ):
        go(msend2_ref.at[(z + k) % NZ], mrecv2_ref.at[z], m2_send.at[k - 1], m2_recv.at[k - 1], (0, 0, k))
    mrecv2_ref[z] = msend2_ref[z]

    potential_ref[...] = jnp.zeros_like(potential_ref)
    for k, dr in enumerate((-1, 1)):
        slot = dland2_ref.at[k]
        remote(slot, slot, d2_send.at[k], d2_recv.at[k], (dr, 0, 0)).wait_recv()
    for dr in (-1, 0, 1):
        i = x + 4 * (1 - dr)
        base = 4 * (region + dr - 1)
        for delta in range(ND):
            cols = row_tile(base + (i + delta) % WT)
            if dr == 0:
                strip = part_ref[x, z, ND + delta]
            else:
                strip = dland2_ref[(1 - dr) // 2, delta]
            potential_ref[:, cols] += strip
    for k in range(1, NZ):
        slot = mrecv2_ref.at[(z - k + NZ) % NZ]
        remote(slot, slot, m2_send.at[k - 1], m2_recv.at[k - 1], (0, 0, k)).wait_recv()
    back = []
    for grp in range(2):
        back += swap_groups([mrecv2_ref[zz, grp] for zz in range(NZ)])
    for delta in range(1, 6):
        for wrap in range(2):
            cols = row_tile(my_tile - delta + WT * wrap)
            potential_ref[:, cols] += back[2 * (delta - 1) + wrap]

    for copy in sent:
        copy.wait_send()


def on_device(density_matrix, basis, union, weights, in_scale, in_shift, hidden_weight, hidden_bias, out_weight):
    vmem = pl.BlockSpec(memory_space=pltpu.VMEM)
    f32, bf16 = jnp.float32, jnp.bfloat16
    dma = pltpu.SemaphoreType.DMA
    count = len(CLASSES) * NN
    scratch = [
        pltpu.VMEM((2, PB, U * TILE), f32),
        pltpu.VMEM((NP, WIDE), f32),
        pltpu.VMEM((NPAIR, NP, 768), bf16),
        pltpu.VMEM((WT * TILE, NP), bf16),
        pltpu.VMEM((WT * TILE, NP), bf16),
        pltpu.VMEM((NP, WIDE), bf16),
        pltpu.VMEM((NP, WIDE), bf16),
        pltpu.VMEM((768, SPAN), bf16),
        pltpu.VMEM((NX, NZ, STRIPS, ROWS, TILE), f32),
        pltpu.VMEM((NX, NZ, STRIPS, ROWS, TILE), f32),
        pltpu.VMEM((NN, STRIPS, ROWS, TILE), f32),
        pltpu.VMEM((STRIPS, ROWS, TILE), f32),
        pltpu.VMEM((NZ, 2, ROWS, TILE), f32),
        pltpu.VMEM((NZ, 2, ROWS, TILE), f32),
        pltpu.VMEM((10, ROWS, TILE), f32),
        pltpu.VMEM((2, ND, ROWS, TILE), f32),
        pltpu.VMEM((2, ND, ROWS, TILE), f32),
        pltpu.VMEM((15, ROWS, TILE), f32),
        pltpu.VMEM((NZ, 2, ROWS, TILE), f32),
        pltpu.VMEM((NZ, 2, ROWS, TILE), f32),
        pltpu.VMEM((16, ROWS, TILE), f32),
        pltpu.VMEM((2, ND, ROWS, TILE), f32),
        pltpu.VMEM((15, ROWS, TILE), f32),
        dma, dma((count,)), dma((count,)), dma((count,)), dma((count,)),
        dma((NZ - 1,)), dma((NZ - 1,)), dma((2,)), dma((2,)), dma((15,)), dma((15,)),
        dma((NZ - 1,)), dma((NZ - 1,)), dma((2,)), dma((2,)), dma((15,)), dma((15,)),
    ]
    density, potential = pl.pallas_call(
        kernel,
        out_shape=(
            jax.ShapeDtypeStruct(weights.shape, f32),
            jax.ShapeDtypeStruct(density_matrix.shape, f32),
        ),
        in_specs=[
            pl.BlockSpec(memory_space=pltpu.SMEM), vmem, pl.BlockSpec(memory_space=pl.ANY),
            vmem, vmem, vmem, vmem, vmem, vmem,
        ],
        out_specs=(vmem, vmem),
        scratch_shapes=scratch,
        compiler_params=pltpu.CompilerParams(
            collective_id=0, has_side_effects=True, vmem_limit_bytes=66_000_000
        ),
    )(
        union, density_matrix, basis, weights,
        in_scale[None], in_shift[None], hidden_weight, hidden_bias[None], out_weight[None],
    )
    return density, potential


def solution(mesh):
    own = P(("space", "dev"), None)
    in_specs = (own, P(("space", "dev"), None, None), own, own, P(), P(), P(), P(), P())
    return jax.shard_map(on_device, mesh=mesh, in_specs=in_specs, out_specs=(own, own), check_vma=False)
```

profile of v0, /device:TPU:1, one launch (start us, length us, event | category | flops | bytes accessed | tf_op | source)
XLA Modules:
  0.0 134.9 jit_solution(1219670294803015880)
XLA Ops:
  0.6 131.3 %shard_map.104 = (f32[2,384]{1,0:T(2,128)}, f32[16,4096]{1,0:T(8,128)}) custom-call(s32[2,8]{1,0:T(2,128)} %union_ref.1, f32[16,4096]{1,0:T(8,128)} %rows_ref.1, f32[2,384,1024]{2,1,0:T(8,128)} %basis_hbm.1, f32[2,384]{1,0:T(2,128)} %weights_ref.1, f32[1,256]{1,0:T(1,128)} %bitcast.4, f32[1,256]{1,0:T(1,128)} %bitcast.5, f32[256,256]{1,0:T(8,128)} %hidden_ref.1, ...), custom_call_target="tpu_custom_call" | custom-call | tf_op jit(solution)/shard_map/pallas_call | solution.py:452
  132.0 1.2 copy.13
  133.2 1.7 %copy.14 = f32[16,4096]{1,0:T(8,128)} copy(f32[16,4096]{1,0:T(8,128)} %get-tuple-element.5) | data formatting | bytes 524288
where the time goes:
time: 135 us
  Pallas kernels  131 us (97%)
  local copies, waits for them, and re-layouts  2.92 us (2%)
    pallas_call x1, Pallas kernels, on_device(): pl.pallas_call(kernel, out_shape=(jax.ShapeDtypeStruct(weights.shape, f32...  131 us
    unnamed x2, local copies, waits for them, and re-layouts  2.92 us

commit v1 on v0

v1 whole, which is shorter than its diff:
```python
import heapq

import jax
import jax.numpy as jnp
from jax import lax
from jax.experimental import pallas as pl
from jax.experimental.pallas import tpu as pltpu
from jax.sharding import PartitionSpec as P

MESH = pl.DeviceIdType.MESH
TILE = 128
U = 8
NX, NZ = 4, 8
NS = 8
ROWS = 16
REG = 4 * TILE
PB = 384
NP = 2 * PB

STRIPS = 16
FAR = 11
SHARED = STRIPS - FAR

CLASSES = (
    (FAR, STRIPS, True, 1),
    (0, 5, True, -1),
    (5, 8, False, 1),
    (8, FAR, False, -1),
)


def class_nodes(sign):
    xs = (0, 1, -1, 2 * sign)
    zs = (0, 1, -1, 2, -2, 3, -3, 4 * sign)
    return [(dx, dz) for dx in xs for dz in zs if (dx, dz) != (0, 0)]


def parent_of(node, z_first):
    dx, dz = node
    step_x = (dx > 0) - (dx < 0)
    step_z = (dz > 0) - (dz < 0)
    if z_first:
        return ((dx - step_x, dz), (step_x, 0)) if dx else ((0, dz - step_z), (0, step_z))
    return ((dx, dz - step_z), (0, step_z)) if dz else ((dx - step_x, 0), (step_x, 0))


def plan(latency=11.0, ahead=12.0):
    children = {}
    for c, (lo, hi, z_first, sign) in enumerate(CLASSES):
        for node in class_nodes(sign):
            par, step = parent_of(node, z_first)
            children.setdefault((c, par), []).append((c, node, step))

    def depth(c, node):
        return 1 + max((depth(c, kid[1]) for kid in children.get((c, node), [])), default=0)

    rank_z, rank_x = (0, 1, 2, 3), (2, 3, 0, 1)
    waiting = {}
    free = {}
    events = []
    issue = []
    arrive = {}
    count = 0

    def offer(now, kids):
        nonlocal count
        for c, node, step in kids:
            rank = (rank_z if step[1] else rank_x)[c]
            count += 1
            heapq.heappush(waiting.setdefault(step, []), (rank, -depth(c, node), count, now, c, node, step))
            count += 1
            heapq.heappush(events, (max(now, free.get(step, 0.0)), count, step, None))

    for c in range(len(CLASSES)):
        offer(0.0, children[(c, (0, 0))])
    while events:
        now, _, step, landed = heapq.heappop(events)
        if landed is not None:
            offer(now, children.get(landed, []))
            continue
        if free.get(step, 0.0) > now or not waiting[step]:
            continue
        _, _, _, ready, c, node, step = heapq.heappop(waiting[step])
        size = CLASSES[c][1] - CLASSES[c][0]
        free[step] = now + size
        arrive[(c, node)] = now + size + latency
        issue.append((max(ready, now - ahead), len(issue), c, node, step))
        count += 1
        heapq.heappush(events, (arrive[(c, node)], count, step, (c, node)))
        count += 1
        heapq.heappush(events, (free[step], count, step, None))
    return sorted(issue), arrive, children


ISSUE, ARRIVE, CHILDREN = plan()
STEP = {(c, node): step for _, _, c, node, step in ISSUE}
PARENT = {kid[:2]: par for par, kids in CHILDREN.items() for kid in kids}
BACK = sorted(STEP, key=lambda key: -ARRIVE[key])
NN = NX * NZ - 1
NODE_ID = {}
for _c in range(len(CLASSES)):
    for _k, _node in enumerate(class_nodes(CLASSES[_c][3])):
        NODE_ID[(_c, _node)] = _k
X_STEPS = (0, 1, -1, 2)


def split(value):
    high = value.astype(jnp.bfloat16)
    low = (value - high.astype(jnp.float32)).astype(jnp.bfloat16)
    return high, low


def swap_groups(parts):
    lane = lax.broadcasted_iota(jnp.int32, (ROWS, TILE), 1) // ROWS
    parts = list(parts)
    for bit in range(3):
        d = 1 << bit
        upper = (lane // d) % 2 == 1
        for i in range(8):
            if i & d:
                continue
            a, b = parts[i], parts[i + d]
            parts[i] = jnp.where(upper, pltpu.roll(b, ROWS * d, 1), a)
            parts[i + d] = jnp.where(upper, b, pltpu.roll(a, TILE - ROWS * d, 1))
    return parts


def fdot(a, b):
    return jnp.dot(a, b, preferred_element_type=jnp.float32)


def kernel(
    union_ref, rows_ref, basis_hbm, weights_ref, scale_ref, shift_ref, hidden_ref, bias_ref, out_w_ref,
    density_ref, potential_ref,
    basis_ref, full_ref, v3_ref, bth_ref, btl_ref, sh_ref, sl_ref, t3_ref, acc_ref, res_ref,
    gath_ref, gath2_ref, part_ref, part2_ref, land_ref, land2_ref,
    msend_ref, mrecv_ref, tt_ref, dsend_ref, dland_ref, tland_ref, mine_ref,
    msend2_ref, mrecv2_ref, ss_ref, dland2_ref, tland2_ref,
    basis_sem, ag_send, ag_recv, rs_send, rs_recv, pa_send, pa_recv, pr_send, pr_recv,
    m_send, m_recv, d_send, d_recv, t_send, t_recv,
    m2_send, m2_recv, d2_send, d2_recv, t2_send, t2_recv,
):
    region = lax.axis_index("space")
    dev = lax.axis_index("dev")
    x = dev // NZ
    z = dev % NZ
    core = region % 2
    sigma = 1 - 2 * core

    def at(offset):
        return (region + offset + 2 * NS) % NS

    outer, partner = at(-sigma), at(sigma)
    beyond = at(-2 * sigma)
    past = at(2 * sigma)

    def xof(d):
        return (x + d + 2 * NX) % NX

    def zof(d):
        return (z + d + 2 * NZ) % NZ

    def target(reg, xx, zz):
        return {"space": reg, "dev": xx * NZ + zz}

    load = pltpu.make_async_copy(basis_hbm, basis_ref, basis_sem)
    load.start()

    barrier = pltpu.get_barrier_semaphore()
    peers = [target(region, x, zof(d)) for d in range(1, NZ)]
    peers += [target(region, xof(d), z) for d in range(1, NX)]
    peers += [target(outer, xof(d), z) for d in range(NX)]
    peers += [target(partner, xof(d), z) for d in range(NX)]
    for peer in peers:
        pl.semaphore_signal(barrier, inc=1, device_id=peer, device_id_type=MESH)

    sent = []

    def remote(src, dst, send_sem, recv_sem, where):
        return pltpu.make_async_remote_copy(
            src_ref=src, dst_ref=dst, send_sem=send_sem, recv_sem=recv_sem,
            device_id=where, device_id_type=MESH,
        )

    def go(*args):
        copy = remote(*args)
        copy.start()
        sent.append(copy)

    def landed(slot, send_sem, recv_sem, where):
        remote(slot, slot, send_sem, recv_sem, where).wait_recv()

    def row_tile(reg, tile):
        return pl.ds(pl.multiple_of(reg * REG + tile * TILE, TILE), TILE)

    for d in range(3):
        strip = rows_ref[:, row_tile(region, xof(d))]
        dsend_ref[d] = strip
        mine_ref[FAR + d] = strip
    for j in range(4):
        dsend_ref[3 + j] = rows_ref[:, row_tile(outer, j)]
        dsend_ref[7 + j] = rows_ref[:, row_tile(beyond, j)]
    for e in range(2):
        mine_ref[FAR + 3 + e] = rows_ref[:, row_tile(partner, xof(core + e))]

    def transposed_columns():
        cols = [row_tile(region, xof(-1))]
        cols += [row_tile(outer, j) for j in range(4)]
        cols += [row_tile(past, j) for j in range(4)]
        cols += [row_tile(partner, xof(core - 1 - e)) for e in range(2)]
        return cols

    slots = [rows_ref[:, cols] for cols in transposed_columns()]
    zero = jnp.zeros((ROWS, TILE), jnp.float32)
    slots += [zero] * (16 - len(slots))
    for grp in range(2):
        for zz, part in enumerate(swap_groups(slots[8 * grp : 8 * grp + 8])):
            msend_ref[zz, grp] = part

    pl.semaphore_wait(barrier, len(peers))
    for k in range(1, NZ):
        go(msend_ref.at[zof(k)], mrecv_ref.at[z], m_send.at[k - 1], m_recv.at[k - 1], target(region, x, zof(k)))
    go(dsend_ref, dland_ref, d_send, d_recv, target(outer, x, z))
    mrecv_ref[z] = msend_ref[z]
    t3_ref[...] = jnp.zeros_like(t3_ref)
    acc_ref[...] = jnp.zeros_like(acc_ref)

    for k in range(1, NZ):
        landed(mrecv_ref.at[zof(-k)], m_send.at[k - 1], m_recv.at[k - 1], target(region, x, zof(k)))
    for grp in range(2):
        stacked = mrecv_ref[:, grp].reshape(TILE, TILE).T
        for e in range(8):
            tt_ref[8 * grp + e] = stacked[ROWS * e : ROWS * (e + 1)]

    kinds = [(0, outer, xof(-1), 1)]
    kinds += [(1 + xof(-d), region, xof(-d), 3 + xof(d)) for d in range(NX)]
    kinds += [(5 + xof(-d), partner, xof(-d), 7 + xof(d)) for d in range(NX)]
    kinds += [(0, region, xof(-1), FAR + 1)]
    kinds += [(9 + e, partner, xof(core - 1 - e), FAR + 3 + e) for e in range(2)]
    local = 1
    for k, (slot, reg, xx, _) in enumerate(kinds):
        if k == local:
            tland_ref[k] = tt_ref[slot]
        else:
            go(tt_ref.at[slot], tland_ref.at[k], t_send.at[k], t_recv.at[k], target(reg, xx, z))

    landed(dland_ref, d_send, d_recv, target(outer, x, z))
    mine_ref[0:FAR] = dland_ref[...]
    for k, (_, reg, xx, strip) in enumerate(kinds):
        if k != local:
            landed(tland_ref.at[k], t_send.at[k], t_recv.at[k], target(reg, xx, z))
        mine_ref[strip] += tland_ref[k]
    gath_ref[x, z] = mine_ref[...]

    beside = {
        step: target(region, xof(step[0]), zof(step[1])) for step in ((1, 0), (-1, 0), (0, 1), (0, -1))
    }
    against = {step: beside[(-step[0], -step[1])] for step in beside}
    other_core = target(partner, x, z)

    def block(ref, c, node):
        lo, hi = CLASSES[c][:2]
        return ref.at[xof(-node[0]), zof(-node[1]), lo:hi]

    done = {(c, (0, 0)) for c in range(len(CLASSES))}

    def need(c, node):
        if (c, node) not in done:
            done.add((c, node))
            view = block(gath_ref, c, node)
            sem = c * NN + NODE_ID[(c, node)]
            landed(view, ag_send.at[sem], ag_recv.at[sem], beside[STEP[(c, node)]])

    def need_class(c):
        for node in class_nodes(CLASSES[c][3]):
            need(c, node)

    def forward(c, node):
        par = PARENT[(c, node)]
        need(*par)
        view = block(gath_ref, c, par[1])
        sem = c * NN + NODE_ID[(c, node)]
        go(view, view, ag_send.at[sem], ag_recv.at[sem], beside[STEP[(c, node)]])

    def share(k):
        dx = X_STEPS[k]
        for node in [(dx, 0)] + [n for n in class_nodes(CLASSES[0][3]) if n[0] == dx and n[1] != 0]:
            need(0, node)
        go(gath_ref.at[xof(-dx), :, FAR:STRIPS], gath2_ref.at[xof(-dx)], pa_send.at[k], pa_recv.at[k], other_core)

    def shared(k):
        landed(gath2_ref.at[xof(-X_STEPS[k])], pa_send.at[k], pa_recv.at[k], other_core)

    slot_region = (outer, region, partner)

    def prepare(t):
        s, off = t // 4, (t % 4) * TILE
        tile = slot_region[s] * 4 + t % 4
        for b in range(2):
            value = None
            for u in range(U):
                hit = (union_ref[b, u] == tile).astype(jnp.float32)
                term = basis_ref[b, :, u * TILE : (u + 1) * TILE] * hit
                value = term if value is None else value + term
            high, low = split(value)
            rows = slice(b * PB, (b + 1) * PB)
            full_ref[rows, t * TILE : (t + 1) * TILE] = value
            for part, src in enumerate((high, low, high)):
                v3_ref[s, rows, REG * part + off : REG * part + off + TILE] = src
            high_t, low_t = split(value.T)
            bth_ref[t * TILE : (t + 1) * TILE, rows] = high_t
            btl_ref[t * TILE : (t + 1) * TILE, rows] = low_t

    def lanes(tile):
        return pl.ds(pl.multiple_of(tile * TILE, TILE), TILE)

    def unit_tiles(r, c):
        ref, base = ((gath_ref, 0), (gath_ref, FAR), (gath2_ref, 0))[r]
        for xx in range(NX):
            if r == c:
                yield from ((xx, slice((xx + d) % NX * TILE, ((xx + d) % NX + 1) * TILE), base + d) for d in range(3))
            elif r == 0:
                yield from ((xx, slice(j * TILE, (j + 1) * TILE), (3, 7)[c - 1] + j) for j in range(4))
            else:
                first = core if r == 1 else 1 - core
                yield from ((xx, lanes((xx + first + e) % NX), base + 3 + e) for e in range(2))

    def density_unit(r, c):
        ref = gath2_ref if r == 2 else gath_ref
        blank = jnp.zeros((TILE, TILE), jnp.bfloat16)

        def put(xx, cols, high, low):
            for part, src in enumerate((high, high, low)):
                t3_ref[REG * part + TILE * xx : REG * part + TILE * (xx + 1), cols] = src

        for xx, cols, strip in unit_tiles(r, c):
            put(xx, cols, *split(ref[xx, :, strip].reshape(TILE, TILE)))
        if r == c:
            for xx in range(NX):
                j = (xx + 3) % NX
                put(xx, slice(j * TILE, (j + 1) * TILE), blank, blank)
        elif r > 0:
            first = core if r == 1 else 1 - core
            for xx in range(NX):
                for e in (2, 3):
                    put(xx, lanes((xx + first + e) % NX), blank, blank)
        for q in range(2):
            res = fdot(v3_ref[r], t3_ref[:, 256 * q : 256 * (q + 1)])
            res = res * full_ref[:, REG * c + 256 * q : REG * c + 256 * (q + 1)]
            acc_ref[...] += res[:, :TILE] + res[:, TILE:]

    agenda = [(key, n, "send", (c, node)) for key, n, c, node, _ in ISSUE]
    for k, dx in enumerate(X_STEPS):
        key = max(ARRIVE[(0, n)] for n in class_nodes(CLASSES[0][3]) if n[0] == dx)
        agenda.append((key, k, "share", k))
    first_done, *ends = [max(ARRIVE[key] for key in STEP if key[0] == c) for c in range(len(CLASSES))]
    for t in range(12):
        agenda.append((4.0 + t * (first_done - 8.0) / 12, t, "prepare", (4, 5, 6, 7, 8, 9, 10, 11, 0, 1, 2, 3)[t]))
    agenda.append((first_done + 0.1, 0, "unit", (1, 1)))
    agenda.append((first_done + 10, 1, "unit", (1, 2)))
    agenda.append((first_done + 20, 2, "unit", (2, 1)))
    agenda.append((first_done + 30, 3, "unit", (2, 2)))
    for key, _, what, arg in sorted(agenda, key=lambda a: (a[0], a[2], a[1])):
        if what == "send":
            forward(*arg)
        elif what == "share":
            share(arg)
        elif what == "prepare":
            if arg == 4:
                load.wait()
            prepare(arg)
        else:
            if arg == (1, 1):
                need_class(0)
            if arg == (2, 1):
                for k in range(len(X_STEPS)):
                    shared(k)
            density_unit(*arg)
    if ends[2] < ends[0]:
        need_class(2)
        need_class(3)
        density_unit(0, 2)
        need_class(1)
    else:
        need_class(1)
        density_unit(0, 0)
        need_class(2)
        density_unit(0, 1)
        need_class(3)
        density_unit(0, 2)
    if ends[2] < ends[0]:
        density_unit(0, 0)
        density_unit(0, 1)
    rho = jnp.sum(acc_ref[...], axis=1, keepdims=True)

    hid_high, hid_low = split(hidden_ref[...])
    first = jnp.tanh(rho * scale_ref[...] + shift_ref[...])
    high, low = split(first)
    pre = fdot(high, hid_high) + fdot(low, hid_high) + fdot(high, hid_low) + bias_ref[...]
    second = pre / (1.0 + jnp.exp(-pre))
    pot = jnp.sum(second * out_w_ref[...], axis=1, keepdims=True)
    factors = []
    for b in range(2):
        rho_b = jnp.broadcast_to(rho[b * PB : (b + 1) * PB], (PB, TILE)).T
        density_ref[b : b + 1, :] = rho_b[0:1]
        w_b = jnp.broadcast_to(weights_ref[b : b + 1, :], (TILE, PB)).T
        factors.append(w_b[:, 0:1] * pot[b * PB : (b + 1) * PB])

    def scale_slot(s):
        for b in range(2):
            rows = slice(b * PB, (b + 1) * PB)
            for j in range(4):
                cols = slice(REG * s + TILE * j, REG * s + TILE * (j + 1))
                high, low = split(full_ref[rows, cols] * factors[b])
                sh_ref[rows, cols] = high
                sl_ref[rows, cols] = low

    def part_unit(r, c):
        rows = slice(REG * r, REG * (r + 1))
        ref = part2_ref if r == 2 else part_ref
        for q in range(2):
            cols = slice(REG * c + 256 * q, REG * c + 256 * (q + 1))
            right = sh_ref[:, cols]
            res_ref[:, 256 * q : 256 * (q + 1)] = (
                fdot(bth_ref[rows], right) + fdot(btl_ref[rows], right) + fdot(bth_ref[rows], sl_ref[:, cols])
            )
        for xx, cols, strip in unit_tiles(r, c):
            ref[xx, :, strip] = res_ref[TILE * xx : TILE * (xx + 1), cols].reshape(NZ, ROWS, TILE)

    def summed(c, node):
        lo, hi = CLASSES[c][:2]
        bx, bz = xof(-node[0]), zof(-node[1])
        if c == 0:
            if node[0] not in merged:
                merged.add(node[0])
                k = X_STEPS.index(node[0])
                landed(land2_ref.at[bx], pr_send.at[k], pr_recv.at[k], other_core)
            part_ref[bx, bz, lo:hi] += land2_ref[bx, bz]
        for _, kid, step in CHILDREN.get((c, node), []):
            k = NODE_ID[(c, kid)]
            sem = c * NN + k
            landed(land_ref.at[k, lo:hi], rs_send.at[sem], rs_recv.at[sem], against[step])
            part_ref[bx, bz, lo:hi] += land_ref[k, lo:hi]

    merged = set()

    def back(c, node):
        summed(c, node)
        lo, hi = CLASSES[c][:2]
        k = NODE_ID[(c, node)]
        go(
            block(part_ref, c, node), land_ref.at[k, lo:hi],
            rs_send.at[c * NN + k], rs_recv.at[c * NN + k], against[STEP[(c, node)]],
        )

    scale_slot(0)
    part_unit(0, 0)
    scale_slot(1)
    part_unit(0, 1)
    scale_slot(2)
    part_unit(0, 2)
    near = [key for key in BACK if key[0] == 0]
    start = BACK.index(near[0])
    marks = {min(start, 12): "partner", min(start, 30): "own"}
    for n, key in enumerate(BACK):
        what = marks.get(n)
        if what == "partner":
            part_unit(2, 2)
            part_unit(2, 1)
            for k in reversed(range(len(X_STEPS))):
                bx = xof(-X_STEPS[k])
                go(part2_ref.at[bx], land2_ref.at[bx], pr_send.at[k], pr_recv.at[k], other_core)
        elif what == "own":
            part_unit(1, 1)
            part_unit(1, 2)
        back(*key)

    own = part_ref.at[x, z]
    for c in (1, 2, 3):
        summed(c, (0, 0))
    go(own.at[0:FAR], dland2_ref, d2_send, d2_recv, target(outer, x, z))
    returns = [(1, outer, xof(1), 0)]
    returns += [(3 + xof(d), region, xof(d), 1 + xof(-d)) for d in range(NX)]
    returns += [(7 + xof(d), partner, xof(d), 5 + xof(-d)) for d in range(NX)]
    returns += [(FAR + 1, region, xof(1), 0)]
    returns += [(FAR + 3 + e, partner, xof(core + e), 9 + e) for e in range(2)]

    def give(k):
        strip, reg, xx, slot = returns[k]
        if k != local:
            go(own.at[strip], tland2_ref.at[k], t2_send.at[k], t2_recv.at[k], target(reg, xx, z))

    for k in range(9):
        give(k)
    summed(0, (0, 0))
    for k in range(9, 12):
        give(k)
    ss_ref[...] = jnp.zeros_like(ss_ref)
    for k, (strip, reg, xx, slot) in enumerate(returns):
        if k == local:
            ss_ref[slot] += part_ref[x, z, strip]
        else:
            landed(tland2_ref.at[k], t2_send.at[k], t2_recv.at[k], target(reg, xx, z))
            ss_ref[slot] += tland2_ref[k]
    for grp in range(2):
        stacked = ss_ref[8 * grp : 8 * grp + 8].reshape(TILE, TILE).T
        for zz in range(NZ):
            msend2_ref[zz, grp] = stacked[ROWS * zz : ROWS * (zz + 1)]
    for k in range(1, NZ):
        go(msend2_ref.at[zof(k)], mrecv2_ref.at[z], m2_send.at[k - 1], m2_recv.at[k - 1], target(region, x, zof(k)))
    mrecv2_ref[z] = msend2_ref[z]

    potential_ref[...] = jnp.zeros_like(potential_ref)
    for d in range(3):
        potential_ref[:, row_tile(region, xof(d))] += part_ref[x, z, FAR + d]
    for e in range(2):
        potential_ref[:, row_tile(partner, xof(core + e))] += part_ref[x, z, FAR + 3 + e]
    landed(dland2_ref, d2_send, d2_recv, target(outer, x, z))
    for d in range(3):
        potential_ref[:, row_tile(region, xof(d))] += dland2_ref[d]
    for j in range(4):
        potential_ref[:, row_tile(outer, j)] += dland2_ref[3 + j]
        potential_ref[:, row_tile(beyond, j)] += dland2_ref[7 + j]
    for k in range(1, NZ):
        landed(mrecv2_ref.at[zof(-k)], m2_send.at[k - 1], m2_recv.at[k - 1], target(region, x, zof(k)))
    turned = []
    for grp in range(2):
        turned += swap_groups([mrecv2_ref[zz, grp] for zz in range(NZ)])
    for e, cols in enumerate(transposed_columns()):
        potential_ref[:, cols] += turned[e]

    for copy in sent:
        copy.wait_send()


def on_device(density_matrix, basis, union, weights, in_scale, in_shift, hidden_weight, hidden_bias, out_weight):
    vmem = pl.BlockSpec(memory_space=pltpu.VMEM)
    f32, bf16 = jnp.float32, jnp.bfloat16
    dma = pltpu.SemaphoreType.DMA
    count = len(CLASSES) * NN
    strip = (ROWS, TILE)
    scratch = [
        pltpu.VMEM((2, PB, U * TILE), f32),
        pltpu.VMEM((NP, 3 * REG), f32),
        pltpu.VMEM((3, NP, 3 * REG), bf16),
        pltpu.VMEM((3 * REG, NP), bf16),
        pltpu.VMEM((3 * REG, NP), bf16),
        pltpu.VMEM((NP, 3 * REG), bf16),
        pltpu.VMEM((NP, 3 * REG), bf16),
        pltpu.VMEM((3 * REG, REG), bf16),
        pltpu.VMEM((NP, TILE), f32),
        pltpu.VMEM((REG, REG), f32),
        pltpu.VMEM((NX, NZ, STRIPS) + strip, f32),
        pltpu.VMEM((NX, NZ, SHARED) + strip, f32),
        pltpu.VMEM((NX, NZ, STRIPS) + strip, f32),
        pltpu.VMEM((NX, NZ, SHARED) + strip, f32),
        pltpu.VMEM((NN, STRIPS) + strip, f32),
        pltpu.VMEM((NX, NZ, SHARED) + strip, f32),
        pltpu.VMEM((NZ, 2) + strip, f32),
        pltpu.VMEM((NZ, 2) + strip, f32),
        pltpu.VMEM((16,) + strip, f32),
        pltpu.VMEM((FAR,) + strip, f32),
        pltpu.VMEM((FAR,) + strip, f32),
        pltpu.VMEM((12,) + strip, f32),
        pltpu.VMEM((STRIPS,) + strip, f32),
        pltpu.VMEM((NZ, 2) + strip, f32),
        pltpu.VMEM((NZ, 2) + strip, f32),
        pltpu.VMEM((16,) + strip, f32),
        pltpu.VMEM((FAR,) + strip, f32),
        pltpu.VMEM((12,) + strip, f32),
        dma, dma((count,)), dma((count,)), dma((count,)), dma((count,)),
        dma((4,)), dma((4,)), dma((4,)), dma((4,)),
        dma((NZ - 1,)), dma((NZ - 1,)), dma, dma, dma((12,)), dma((12,)),
        dma((NZ - 1,)), dma((NZ - 1,)), dma, dma, dma((12,)), dma((12,)),
    ]
    density, potential = pl.pallas_call(
        kernel,
        out_shape=(
            jax.ShapeDtypeStruct(weights.shape, f32),
            jax.ShapeDtypeStruct(density_matrix.shape, f32),
        ),
        in_specs=[
            pl.BlockSpec(memory_space=pltpu.SMEM), vmem, pl.BlockSpec(memory_space=pl.ANY),
            vmem, vmem, vmem, vmem, vmem, vmem,
        ],
        out_specs=(vmem, vmem),
        scratch_shapes=scratch,
        compiler_params=pltpu.CompilerParams(
            collective_id=0, has_side_effects=True, vmem_limit_bytes=66_000_000
        ),
    )(
        union, density_matrix, basis, weights,
        in_scale[None], in_shift[None], hidden_weight, hidden_bias[None], out_weight[None],
    )
    return density, potential


def solution(mesh):
    own = P(("space", "dev"), None)
    in_specs = (own, P(("space", "dev"), None, None), own, own, P(), P(), P(), P(), P())
    return jax.shard_map(on_device, mesh=mesh, in_specs=in_specs, out_specs=(own, own), check_vma=False)
```

time: 135 us -> 113 us (0.84)
  Pallas kernels: 131 us -> 110 us
    pallas_call x1, Pallas kernels: 131 us -> 110 us  [on_device(): pl.pallas_call(kernel, out_shape=(jax.ShapeDtypeStruct(weights.shape, f32...]
where the time goes in v1:
time: 113 us
  Pallas kernels  110 us (97%)
  local copies, waits for them, and re-layouts  2.92 us (3%)
    pallas_call x1, Pallas kernels, on_device(): pl.pallas_call(kernel, out_shape=(jax.ShapeDtypeStruct(weights.shape, f32...  110 us
    unnamed x2, local copies, waits for them, and re-layouts  2.92 us

profile of v1, /device:TPU:1, one launch (start us, length us, event | category | flops | bytes accessed | tf_op | source)
XLA Modules:
  0.0 113.1 jit_solution(15010383220959940168)
XLA Ops:
  0.6 109.6 %shard_map.104 = (f32[2,384]{1,0:T(2,128)}, f32[16,4096]{1,0:T(8,128)}) custom-call(s32[2,8]{1,0:T(2,128)} %union_ref.1, f32[16,4096]{1,0:T(8,128)} %rows_ref.1, f32[2,384,1024]{2,1,0:T(8,128)} %basis_hbm.1, f32[2,384]{1,0:T(2,128)} %weights_ref.1, f32[1,256]{1,0:T(1,128)} %bitcast.4, f32[1,256]{1,0:T(1,128)} %bitcast.5, f32[256,256]{1,0:T(8,128)} %hidden_ref.1, ...), custom_call_target="tpu_custom_call" | custom-call | tf_op jit(solution)/shard_map/pallas_call | solution.py:576
  110.2 1.2 %copy.13 = f32[2,384]{1,0:T(2,128)} copy(f32[2,384]{1,0:T(2,128)} %get-tuple-element.4) | data formatting | bytes 6144
  111.5 1.7 %copy.14 = f32[16,4096]{1,0:T(8,128)} copy(f32[16,4096]{1,0:T(8,128)} %get-tuple-element.5) | data formatting | bytes 524288

commit v2 on v1

v2 whole, which is shorter than its diff:
```python
import heapq

import jax
import jax.numpy as jnp
from jax import lax
from jax.experimental import pallas as pl
from jax.experimental.pallas import tpu as pltpu
from jax.sharding import PartitionSpec as P

MESH = pl.DeviceIdType.MESH
TILE = 128
U = 8
NX, NZ = 4, 8
NS = 8
ROWS = 16
REG = 4 * TILE
PB = 384
NP = 2 * PB

STRIPS = 11
SHARED = 5
TO_PARTNER = (0, 5)
TO_OUTER = (2, 7)

CLASSES = (
    (0, 4, True, 1),
    (4, 7, True, -1),
    (7, 11, False, -1),
)
LATE = 10.0


def class_nodes(sign):
    xs = (0, 1, -1, 2 * sign)
    zs = (0, 1, -1, 2, -2, 3, -3, 4 * sign)
    return [(dx, dz) for dx in xs for dz in zs if (dx, dz) != (0, 0)]


def parent_of(node, z_first):
    dx, dz = node
    step_x = (dx > 0) - (dx < 0)
    step_z = (dz > 0) - (dz < 0)
    if z_first:
        return ((dx - step_x, dz), (step_x, 0)) if dx else ((0, dz - step_z), (0, step_z))
    return ((dx, dz - step_z), (0, step_z)) if dz else ((dx - step_x, 0), (step_x, 0))


def plan(latency=11.0, ahead=12.0):
    children = {}
    for c, (lo, hi, z_first, sign) in enumerate(CLASSES):
        for node in class_nodes(sign):
            par, step = parent_of(node, z_first)
            children.setdefault((c, par), []).append((c, node, step))

    def depth(c, node):
        return 1 + max((depth(c, kid[1]) for kid in children.get((c, node), [])), default=0)

    waiting = {}
    free = {}
    events = []
    issue = []
    arrive = {}
    count = 0

    def offer(now, kids):
        nonlocal count
        for c, node, step in kids:
            if step[1]:
                rank = (0, 1, 2)[c]
            else:
                rank = (1, 1, 0)[c] + (abs(node[0]) > 1)
            count += 1
            heapq.heappush(waiting.setdefault(step, []), (rank, -depth(c, node), count, now, c, node, step))
            count += 1
            heapq.heappush(events, (max(now, free.get(step, 0.0)), count, step, None))

    for c in range(len(CLASSES)):
        count += 1
        heapq.heappush(events, (LATE if c == 2 else 0.0, count, None, (c, (0, 0))))
    while events:
        now, _, step, landed = heapq.heappop(events)
        if landed is not None:
            offer(now, children.get(landed, []))
            continue
        if free.get(step, 0.0) > now or not waiting[step]:
            continue
        _, _, _, ready, c, node, step = heapq.heappop(waiting[step])
        size = CLASSES[c][1] - CLASSES[c][0]
        free[step] = now + size
        arrive[(c, node)] = now + size + latency
        issue.append((max(ready, now - ahead), len(issue), c, node, step))
        count += 1
        heapq.heappush(events, (arrive[(c, node)], count, step, (c, node)))
        count += 1
        heapq.heappush(events, (free[step], count, step, None))
    return sorted(issue), arrive, children


ISSUE, ARRIVE, CHILDREN = plan()
STEP = {(c, node): step for _, _, c, node, step in ISSUE}
PARENT = {kid[:2]: par for par, kids in CHILDREN.items() for kid in kids}
BACK = sorted(STEP, key=lambda key: -ARRIVE[key])
NN = NX * NZ - 1
NODE_ID = {}
NODE_AT = {}
for _c in range(len(CLASSES)):
    NODE_AT[(_c, 0, 0)] = (0, 0)
    for _k, _node in enumerate(class_nodes(CLASSES[_c][3])):
        NODE_ID[(_c, _node)] = _k
        NODE_AT[(_c, _node[0] % NX, _node[1] % NZ)] = _node
PAIRS = ((0, 1), (3, 2))


def split(value):
    high = value.astype(jnp.bfloat16)
    low = (value - high.astype(jnp.float32)).astype(jnp.bfloat16)
    return high, low


def swap_groups(parts):
    lane = lax.broadcasted_iota(jnp.int32, (ROWS, TILE), 1) // ROWS
    parts = list(parts)
    for bit in range(3):
        d = 1 << bit
        upper = (lane // d) % 2 == 1
        for i in range(8):
            if i & d:
                continue
            a, b = parts[i], parts[i + d]
            parts[i] = jnp.where(upper, pltpu.roll(b, ROWS * d, 1), a)
            parts[i + d] = jnp.where(upper, b, pltpu.roll(a, TILE - ROWS * d, 1))
    return parts


def fdot(a, b):
    return jnp.dot(a, b, preferred_element_type=jnp.float32)


def kernel(
    union_ref, rows_hbm, basis_hbm, weights_hbm, scale_hbm, shift_hbm, hidden_hbm, bias_hbm, out_w_hbm,
    density_ref, potential_ref,
    rows_ref, basis_ref, weights_ref, scale_ref, shift_ref, hidden_ref, bias_ref, out_w_ref,
    full_ref, v3_ref, bth_ref, btl_ref, sh_ref, sl_ref, t3_ref, acc_ref, res_ref,
    gath_ref, gath2_ref, gath0_ref, part_ref, part2_ref, part0_ref, land_ref, land2_ref, land0_ref,
    msend_ref, mrecv_ref, turn_ref, dland_ref, pland_ref,
    msend2_ref, mrecv2_ref, ss_ref, dland2_ref, pland2_ref,
    load_sem, ag_send, ag_recv, rs_send, rs_recv,
    pa_send, pa_recv, pr_send, pr_recv, oa_send, oa_recv, or_send, or_recv,
    m_send, m_recv, d_send, d_recv, p_send, p_recv,
    m2_send, m2_recv, d2_send, d2_recv, p2_send, p2_recv,
):
    region = lax.axis_index("space")
    dev = lax.axis_index("dev")
    x = dev // NZ
    z = dev % NZ
    core = region % 2
    sigma = 1 - 2 * core

    def at(offset):
        return (region + offset + 2 * NS) % NS

    outer, partner = at(-sigma), at(sigma)
    beyond = at(-2 * sigma)
    past = at(2 * sigma)

    def xof(d):
        return (x + d + 2 * NX) % NX

    def zof(d):
        return (z + d + 2 * NZ) % NZ

    def target(reg, xx, zz):
        return {"space": reg, "dev": xx * NZ + zz}

    loads = []
    for k, (src, dst) in enumerate(
        (
            (rows_hbm, rows_ref), (basis_hbm, basis_ref), (weights_hbm, weights_ref), (scale_hbm, scale_ref),
            (shift_hbm, shift_ref), (hidden_hbm, hidden_ref), (bias_hbm, bias_ref), (out_w_hbm, out_w_ref),
        )
    ):
        copy = pltpu.make_async_copy(src, dst, load_sem.at[k])
        copy.start()
        loads.append(copy)

    barrier = pltpu.get_barrier_semaphore()
    peers = [target(region, x, zof(d)) for d in range(1, NZ)]
    peers += [target(region, xof(d), z) for d in range(1, NX)]
    peers += [target(outer, xof(d), z) for d in range(NX)]
    peers += [target(partner, xof(d), z) for d in range(NX)]
    for peer in peers:
        pl.semaphore_signal(barrier, inc=1, device_id=peer, device_id_type=MESH)

    sent = []

    def remote(src, dst, send_sem, recv_sem, where):
        return pltpu.make_async_remote_copy(
            src_ref=src, dst_ref=dst, send_sem=send_sem, recv_sem=recv_sem,
            device_id=where, device_id_type=MESH,
        )

    def go(*args):
        copy = remote(*args)
        copy.start()
        sent.append(copy)

    def landed(slot, send_sem, recv_sem, where):
        remote(slot, slot, send_sem, recv_sem, where).wait_recv()

    def row_tile(reg, tile):
        return pl.ds(pl.multiple_of(reg * REG + tile * TILE, TILE), TILE)

    own_cols = [row_tile(region, xof(1))]
    own_cols += [row_tile(partner, xof(core + e)) for e in range(2)]
    own_cols += [row_tile(outer, xof(core + e)) for e in range(2)]
    past_cols = [row_tile(past, i) for i in range(NX)]
    loads[0].wait()
    zero = jnp.zeros((ROWS, TILE), jnp.float32)
    for grp, cols in enumerate((own_cols, past_cols)):
        slots = [rows_ref[:, c] for c in cols]
        for zz, part in enumerate(swap_groups(slots + [zero] * (8 - len(slots)))):
            msend_ref[grp, zz] = part

    pl.semaphore_wait(barrier, len(peers))
    for grp in range(2):
        for k in range(1, NZ):
            go(
                msend_ref.at[grp, zof(k)], mrecv_ref.at[grp, z], m_send.at[grp, k - 1], m_recv.at[grp, k - 1],
                target(region, x, zof(k)),
            )
        if grp == 0:
            direct = [(region, xof(-1), row_tile(region, xof(-1)), 0), (region, xof(-2), row_tile(region, xof(-2)), 1)]
            direct += [(partner, xof(core - 1 - e), row_tile(partner, xof(core - 1 - e)), 2 + e) for e in range(2)]
            direct += [(outer, xof(core - 1 - e), row_tile(outer, xof(core - 1 - e)), 4 + e) for e in range(2)]
            direct += [(outer, xof(d), row_tile(beyond, xof(d)), 6 + x) for d in range(NX)]
            for k, (reg, xx, cols, slot) in enumerate(direct):
                go(rows_ref.at[:, cols], dland_ref.at[slot], d_send.at[k], d_recv.at[k], target(reg, xx, z))
    for grp in range(2):
        mrecv_ref[grp, z] = msend_ref[grp, z]

    def arrived(k):
        slot = k if k < 6 else 6 + xof(-(k - 6))
        reg, xx = direct[k][:2]
        landed(dland_ref.at[slot], d_send.at[k], d_recv.at[k], target(reg, xx, z))

    def turned_in(grp):
        for k in range(1, NZ):
            landed(
                mrecv_ref.at[grp, zof(-k)], m_send.at[grp, k - 1], m_recv.at[grp, k - 1], target(region, x, zof(k))
            )
        return mrecv_ref[grp].reshape(TILE, TILE).T

    acc_ref[...] = jnp.zeros_like(acc_ref)
    turned = turned_in(0)

    def turned_strip(e):
        return turned[ROWS * e : ROWS * (e + 1)]

    for k in range(6):
        arrived(k)
    gath_ref[x, z, 2] = rows_ref[:, row_tile(region, x)]
    gath_ref[x, z, 3] = dland_ref[0] + turned_strip(0)
    gath_ref[x, z, 4] = dland_ref[1]
    for e in range(2):
        gath_ref[x, z, e] = dland_ref[2 + e] + turned_strip(1 + e)
        gath_ref[x, z, 5 + e] = dland_ref[4 + e] + turned_strip(3 + e)

    beside = {
        step: target(region, xof(step[0]), zof(step[1])) for step in ((1, 0), (-1, 0), (0, 1), (0, -1))
    }
    against = {step: beside[(-step[0], -step[1])] for step in beside}
    other_core = target(partner, x, z)
    other_chip = target(outer, x, z)

    def block(ref, c, node):
        lo, hi = CLASSES[c][:2]
        return ref.at[xof(-node[0]), zof(-node[1]), lo:hi]

    done = {(c, (0, 0)) for c in range(len(CLASSES))}

    def need(c, node):
        if (c, node) not in done:
            done.add((c, node))
            view = block(gath_ref, c, node)
            sem = c * NN + NODE_ID[(c, node)]
            landed(view, ag_send.at[sem], ag_recv.at[sem], beside[STEP[(c, node)]])

    def forward(c, node):
        par = PARENT[(c, node)]
        need(*par)
        view = block(gath_ref, c, par[1])
        sem = c * NN + NODE_ID[(c, node)]
        go(view, view, ag_send.at[sem], ag_recv.at[sem], beside[STEP[(c, node)]])

    def need_block(ax, az):
        need(0, NODE_AT[(0, ax, az)])
        need(1, NODE_AT[(1, ax, az)])

    def to_partner(ax):
        for az in range(NZ):
            need_block(ax, az)
        bx = xof(-ax)
        lo, hi = TO_PARTNER
        go(gath_ref.at[bx, :, lo:hi], gath2_ref.at[bx], pa_send.at[ax], pa_recv.at[ax], other_core)

    def to_outer(ax, az):
        need_block(ax, az)
        bx, bz = xof(-ax), zof(-az)
        lo, hi = TO_OUTER
        k = ax * NZ + az
        go(gath_ref.at[bx, bz, lo:hi], gath0_ref.at[bx, bz], oa_send.at[k], oa_recv.at[k], other_chip)

    def from_partner(ax):
        landed(gath2_ref.at[xof(-ax)], pa_send.at[ax], pa_recv.at[ax], other_core)

    def from_outer(ax, az):
        k = ax * NZ + az
        landed(gath0_ref.at[xof(-ax), zof(-az)], oa_send.at[k], oa_recv.at[k], other_chip)

    def start_late():
        late = turned_in(1)
        for i in range(NX):
            turn_ref[i] = late[ROWS * i : ROWS * (i + 1)]
        go(turn_ref, pland_ref, p_send, p_recv, other_core)
        for k in range(6, 10):
            arrived(k)
        landed(pland_ref, p_send, p_recv, other_core)
        gath_ref[x, z, 7:11] = dland_ref[6:10] + pland_ref[...]

    slot_region = (outer, region, partner)

    def prepare(t):
        s, off = t // 4, (t % 4) * TILE
        tile = slot_region[s] * 4 + t % 4
        for b in range(2):
            value = None
            for u in range(U):
                hit = (union_ref[b, u] == tile).astype(jnp.float32)
                term = basis_ref[b, :, u * TILE : (u + 1) * TILE] * hit
                value = term if value is None else value + term
            high, low = split(value)
            rows = slice(b * PB, (b + 1) * PB)
            full_ref[rows, t * TILE : (t + 1) * TILE] = value
            for part, src in enumerate((high, low, high)):
                v3_ref[s, rows, REG * part + off : REG * part + off + TILE] = src
            high_t, low_t = split(value.T)
            bth_ref[t * TILE : (t + 1) * TILE, rows] = high_t
            btl_ref[t * TILE : (t + 1) * TILE, rows] = low_t

    def span(base, tile):
        return pl.ds(pl.multiple_of(base + tile * TILE, TILE), TILE)

    def unit_tiles(r, c, xx):
        if r == c:
            base = (0, 2, 2)[r]
            return [((xx + d) % NX, base + d) for d in range(3)], [(xx + 3) % NX]
        if (r, c) == (0, 2):
            return [(i, 7 + i) for i in range(NX)], []
        first = core if c == 1 else 1 - core
        base = {(2, 1): 0, (0, 1): 5, (1, 2): 0, (1, 0): 3}[(r, c)]
        return (
            [((xx + first + e) % NX, base + e) for e in range(2)],
            [(xx + first + e) % NX for e in (2, 3)],
        )

    UNITS = ((1, 1), (2, 1), (0, 1), (2, 2), (1, 2), (0, 0), (1, 0), (0, 2))

    def holder(r, c, own, partners, outers):
        if c == 1 or (r, c) == (0, 2):
            return own
        return partners if c == 2 else outers

    def density_unit(r, c, pair):
        ref = holder(r, c, gath_ref, gath2_ref, gath0_ref)
        blank = jnp.zeros((TILE, TILE), jnp.bfloat16)

        def fill(h, carry):
            xx = xof(-pair[0] - h * (pair[1] - pair[0]))
            held, absent = unit_tiles(r, c, xx)
            cols = span(0, h)
            for row, strip in held:
                high, low = split(ref[xx, :, strip].reshape(TILE, TILE))
                for part, src in enumerate((high, high, low)):
                    t3_ref[span(REG * part, row), cols] = src
            for row in absent:
                for part in range(3):
                    t3_ref[span(REG * part, row), cols] = blank
            return carry

        lax.fori_loop(0, 2, fill, 0)
        res = fdot(v3_ref[r], t3_ref[...])
        for h, ax in enumerate(pair):
            other = full_ref[:, span(REG * c, xof(-ax))]
            acc_ref[...] += res[:, h * TILE : (h + 1) * TILE] * other

    agenda = [(key, n, "send", (c, node)) for key, n, c, node, _ in ISSUE]
    landing = {}
    for ax in range(NX):
        for az in range(NZ):
            landing[(ax, az)] = max(ARRIVE.get((c, NODE_AT[(c, ax, az)]), 0.0) for c in range(2))
            agenda.append((landing[(ax, az)], NZ * ax + az, "outer", (ax, az)))
        agenda.append((max(landing[(ax, az)] for az in range(NZ)) + 0.1, ax, "partner", (ax,)))
    pair_end = max(landing[(ax, az)] for ax in PAIRS[0] for az in range(NZ))
    order = (4, 5, 6, 7, 8, 9, 10, 11, 0, 1, 2, 3)
    for t in range(12):
        agenda.append((6.0 + t * (pair_end - 14.0) / 12, t, "prepare", (order[t],)))
    for n, unit in enumerate(UNITS[:7]):
        agenda.append((pair_end + 1 + 6 * n + (8 if n > 2 else 0) + (8 if n > 4 else 0), n, "unit", unit))
    agenda.append((LATE - 0.5, 0, "late", ()))
    got_partner, got_outer = set(), set()

    def unit_ready(r, c, pair):
        if (r, c) == (0, 2):
            for node in class_nodes(CLASSES[2][3]):
                need(2, node)
            return
        for ax in pair:
            if c == 1:
                for az in range(NZ):
                    need_block(ax, az)
            elif c == 2 and ax not in got_partner:
                got_partner.add(ax)
                from_partner(ax)
            elif c == 0 and ax not in got_outer:
                got_outer.add(ax)
                for az in range(NZ):
                    from_outer(ax, az)

    for key, _, what, arg in sorted(agenda, key=lambda a: (a[0], a[2], a[1])):
        if what == "send":
            forward(*arg)
        elif what == "late":
            start_late()
        elif what == "outer":
            to_outer(*arg)
        elif what == "partner":
            to_partner(*arg)
        elif what == "prepare":
            if arg[0] == order[0]:
                loads[1].wait()
            prepare(*arg)
        else:
            unit_ready(*arg, PAIRS[0])
            density_unit(*arg, PAIRS[0])
    for r, c in UNITS:
        for pair in PAIRS:
            if pair == PAIRS[1] or (r, c) == UNITS[7]:
                unit_ready(r, c, pair)
                density_unit(r, c, pair)
    rho = jnp.sum(acc_ref[...], axis=1, keepdims=True)

    for copy in loads[2:]:
        copy.wait()
    hid_high, hid_low = split(hidden_ref[...])
    first = jnp.tanh(rho * scale_ref[...] + shift_ref[...])
    high, low = split(first)
    pre = fdot(high, hid_high) + fdot(low, hid_high) + fdot(high, hid_low) + bias_ref[...]
    second = pre / (1.0 + jnp.exp(-pre))
    pot = jnp.sum(second * out_w_ref[...], axis=1, keepdims=True)
    factors = []
    for b in range(2):
        rho_b = jnp.broadcast_to(rho[b * PB : (b + 1) * PB], (PB, TILE)).T
        density_ref[b : b + 1, :] = rho_b[0:1]
        w_b = jnp.broadcast_to(weights_ref[b : b + 1, :], (TILE, PB)).T
        factors.append(w_b[:, 0:1] * pot[b * PB : (b + 1) * PB])

    def scale_slot(s):
        for b in range(2):
            rows = slice(b * PB, (b + 1) * PB)
            for j in range(4):
                cols = slice(REG * s + TILE * j, REG * s + TILE * (j + 1))
                high, low = split(full_ref[rows, cols] * factors[b])
                sh_ref[rows, cols] = high
                sl_ref[rows, cols] = low

    def part_unit(r, c, pair):
        rows = slice(REG * r, REG * (r + 1))
        ref = holder(r, c, part_ref, part2_ref, part0_ref)
        tiles = [xof(-ax) for ax in pair]
        right = jnp.concatenate([sh_ref[:, span(REG * c, xx)] for xx in tiles], axis=1)
        right_low = jnp.concatenate([sl_ref[:, span(REG * c, xx)] for xx in tiles], axis=1)
        res_ref[...] = fdot(bth_ref[rows], right) + fdot(btl_ref[rows], right) + fdot(bth_ref[rows], right_low)
        for h, xx in enumerate(tiles):
            for row, strip in unit_tiles(r, c, xx)[0]:
                ref[xx, :, strip] = res_ref[span(0, row), h * TILE : (h + 1) * TILE].reshape(NZ, ROWS, TILE)

    back_partner, back_outer = set(), set()

    def summed(c, node):
        lo, hi = CLASSES[c][:2]
        ax, az = node[0] % NX, node[1] % NZ
        bx, bz = xof(-ax), zof(-az)
        if c < 2:
            if ax not in back_partner:
                back_partner.add(ax)
                landed(land2_ref.at[bx], pr_send.at[ax], pr_recv.at[ax], other_core)
            if (ax, az) not in back_outer:
                back_outer.add((ax, az))
                k = ax * NZ + az
                landed(land0_ref.at[bx, bz], or_send.at[k], or_recv.at[k], other_chip)
        kids = CHILDREN.get((c, node), [])
        for _, kid, step in kids:
            sem = c * NN + NODE_ID[(c, kid)]
            slot = land_ref.at[NODE_ID[(c, kid)], lo:hi]
            landed(slot, rs_send.at[sem], rs_recv.at[sem], against[step])

        def add(i, carry):
            rows = pl.ds(pl.multiple_of(8 * i, 8), 8)
            total = part_ref[bx, bz, lo:hi, rows]
            for _, kid, _ in kids:
                total = total + land_ref[NODE_ID[(c, kid)], lo:hi, rows]
            part_ref[bx, bz, lo:hi, rows] = total
            if c < 2:
                for ref, (first, last) in ((land2_ref, TO_PARTNER), (land0_ref, TO_OUTER)):
                    a, b = max(lo, first), min(hi, last)
                    part_ref[bx, bz, a:b, rows] += ref[bx, bz, a - first : b - first, rows]
            return carry

        if c < 2 or kids:
            lax.fori_loop(0, ROWS // 8, add, 0)

    def back(c, node):
        summed(c, node)
        lo, hi = CLASSES[c][:2]
        k = NODE_ID[(c, node)]
        go(
            block(part_ref, c, node), land_ref.at[k, lo:hi],
            rs_send.at[c * NN + k], rs_recv.at[c * NN + k], against[STEP[(c, node)]],
        )

    def back_to_outer(pair):
        for ax, az in sorted(landing, key=lambda b: -landing[b]):
            if ax in pair:
                bx, bz = xof(-ax), zof(-az)
                k = ax * NZ + az
                go(part0_ref.at[bx, bz], land0_ref.at[bx, bz], or_send.at[k], or_recv.at[k], other_chip)

    def back_to_partner(pair):
        for ax in reversed(pair):
            bx = xof(-ax)
            go(part2_ref.at[bx], land2_ref.at[bx], pr_send.at[ax], pr_recv.at[ax], other_core)

    first_pair, last_pair = PAIRS[1], PAIRS[0]
    scale_slot(0)
    part_unit(0, 0, first_pair)
    part_unit(1, 0, first_pair)
    back_to_outer(first_pair)
    scale_slot(2)
    part_unit(0, 2, first_pair)
    part_unit(0, 2, last_pair)
    near = [key for key in BACK if key[0] < 2]
    far = [key for key in BACK if key[0] == 2]
    for key in far[:8]:
        back(*key)
    rest = [key for key in BACK if key not in far[:8]]
    part_unit(2, 2, first_pair)
    part_unit(1, 2, first_pair)
    back_to_partner(first_pair)
    scale_slot(1)
    for r, c in UNITS[:3]:
        part_unit(r, c, first_pair)
    todo = [
        [((0, 0), (1, 0)), back_to_outer],
        [((2, 2), (1, 2)), back_to_partner],
        [UNITS[:3], None],
    ]
    last_at = min(n for n, key in enumerate(rest) if key[0] < 2 and key[1][0] % NX in last_pair)
    for n, key in enumerate(rest):
        while todo and (n >= 4 + 8 * (3 - len(todo)) or n >= last_at):
            units, after = todo.pop(0)
            for r, c in units:
                part_unit(r, c, last_pair)
            if after is not None:
                after(last_pair)
        back(*key)

    own = part_ref.at[x, z]
    summed(2, (0, 0))
    go(own.at[7:11], pland2_ref, p2_send, p2_recv, other_core)
    returns = [(region, xof(1), 3, 0), (region, xof(2), 4, 1)]
    returns += [(partner, xof(core + e), e, 2 + e) for e in range(2)]
    returns += [(outer, xof(core + e), 5 + e, 4 + e) for e in range(2)]
    returns += [(outer, xof(-d), 7 + xof(-d), 6 + x) for d in range(NX)]

    def give(k):
        reg, xx, strip, slot = returns[k]
        go(own.at[strip], dland2_ref.at[slot], d2_send.at[k], d2_recv.at[k], target(reg, xx, z))

    def turn_back(grp):
        stacked = ss_ref[grp].reshape(TILE, TILE).T
        for zz in range(NZ):
            msend2_ref[grp, zz] = stacked[ROWS * zz : ROWS * (zz + 1)]
        for k in range(1, NZ):
            go(
                msend2_ref.at[grp, zof(k)], mrecv2_ref.at[grp, z], m2_send.at[grp, k - 1], m2_recv.at[grp, k - 1],
                target(region, x, zof(k)),
            )
        mrecv2_ref[grp, z] = msend2_ref[grp, z]

    for k in range(6, 10):
        give(k)
    ss_ref[...] = jnp.zeros_like(ss_ref)
    summed(1, (0, 0))
    summed(0, (0, 0))
    ss_ref[0, 0] = part_ref[x, z, 3]
    for e in range(2):
        ss_ref[0, 1 + e] = part_ref[x, z, e]
        ss_ref[0, 3 + e] = part_ref[x, z, 5 + e]
    turn_back(0)
    for k in range(6):
        give(k)
    landed(pland2_ref, p2_send, p2_recv, other_core)
    ss_ref[1, 0:4] = pland2_ref[...]
    turn_back(1)

    potential_ref[...] = jnp.zeros_like(potential_ref)
    potential_ref[:, row_tile(region, x)] = part_ref[x, z, 2]
    places = [(region, xof(-1)), (region, xof(-2))]
    places += [(partner, xof(core - 1 - e)) for e in range(2)]
    places += [(outer, xof(core - 1 - e)) for e in range(2)]
    places += [(beyond, xof(d)) for d in range(NX)]
    for k, (reg, tile) in enumerate(places):
        slot = k if k < 6 else 6 + xof(k - 6)
        landed(dland2_ref.at[slot], d2_send.at[k], d2_recv.at[k], target(*returns[k][:2], z))
        potential_ref[:, row_tile(reg, tile)] += dland2_ref[slot]
    for grp, cols in enumerate((own_cols, past_cols)):
        for k in range(1, NZ):
            landed(
                mrecv2_ref.at[grp, zof(-k)], m2_send.at[grp, k - 1], m2_recv.at[grp, k - 1],
                target(region, x, zof(k)),
            )
        parts = swap_groups([mrecv2_ref[grp, zz] for zz in range(NZ)])
        for e, c in enumerate(cols):
            potential_ref[:, c] += parts[e]

    for copy in sent:
        copy.wait_send()


def on_device(density_matrix, basis, union, weights, in_scale, in_shift, hidden_weight, hidden_bias, out_weight):
    vmem = pl.BlockSpec(memory_space=pltpu.VMEM)
    hbm = pl.BlockSpec(memory_space=pl.ANY)
    f32, bf16 = jnp.float32, jnp.bfloat16
    dma = pltpu.SemaphoreType.DMA
    count = len(CLASSES) * NN
    strip = (ROWS, TILE)
    width = in_scale.shape[0]
    row = pltpu.VMEM((1, width), f32)
    scratch = [
        pltpu.VMEM(density_matrix.shape, f32),
        pltpu.VMEM((2, PB, U * TILE), f32),
        pltpu.VMEM(weights.shape, f32),
        row, row, pltpu.VMEM((width, width), f32), row, row,
        pltpu.VMEM((NP, 3 * REG), f32),
        pltpu.VMEM((3, NP, 3 * REG), bf16),
        pltpu.VMEM((3 * REG, NP), bf16),
        pltpu.VMEM((3 * REG, NP), bf16),
        pltpu.VMEM((NP, 3 * REG), bf16),
        pltpu.VMEM((NP, 3 * REG), bf16),
        pltpu.VMEM((3 * REG, 2 * TILE), bf16),
        pltpu.VMEM((NP, TILE), f32),
        pltpu.VMEM((REG, 2 * TILE), f32),
        pltpu.VMEM((NX, NZ, STRIPS) + strip, f32),
        pltpu.VMEM((NX, NZ, SHARED) + strip, f32),
        pltpu.VMEM((NX, NZ, SHARED) + strip, f32),
        pltpu.VMEM((NX, NZ, STRIPS) + strip, f32),
        pltpu.VMEM((NX, NZ, SHARED) + strip, f32),
        pltpu.VMEM((NX, NZ, SHARED) + strip, f32),
        pltpu.VMEM((NN, STRIPS) + strip, f32),
        pltpu.VMEM((NX, NZ, SHARED) + strip, f32),
        pltpu.VMEM((NX, NZ, SHARED) + strip, f32),
        pltpu.VMEM((2, NZ) + strip, f32),
        pltpu.VMEM((2, NZ) + strip, f32),
        pltpu.VMEM((4,) + strip, f32),
        pltpu.VMEM((10,) + strip, f32),
        pltpu.VMEM((4,) + strip, f32),
        pltpu.VMEM((2, NZ) + strip, f32),
        pltpu.VMEM((2, NZ) + strip, f32),
        pltpu.VMEM((2, 8) + strip, f32),
        pltpu.VMEM((10,) + strip, f32),
        pltpu.VMEM((4,) + strip, f32),
        dma((8,)), dma((count,)), dma((count,)), dma((count,)), dma((count,)),
        dma((NX,)), dma((NX,)), dma((NX,)), dma((NX,)),
        dma((NX * NZ,)), dma((NX * NZ,)), dma((NX * NZ,)), dma((NX * NZ,)),
        dma((2, NZ - 1)), dma((2, NZ - 1)), dma((10,)), dma((10,)), dma, dma,
        dma((2, NZ - 1)), dma((2, NZ - 1)), dma((10,)), dma((10,)), dma, dma,
    ]
    density, potential = pl.pallas_call(
        kernel,
        out_shape=(
            jax.ShapeDtypeStruct(weights.shape, f32),
            jax.ShapeDtypeStruct(density_matrix.shape, f32),
        ),
        in_specs=[
            pl.BlockSpec(memory_space=pltpu.SMEM), hbm, hbm, hbm, hbm, hbm, hbm, hbm, hbm,
        ],
        out_specs=(vmem, vmem),
        scratch_shapes=scratch,
        compiler_params=pltpu.CompilerParams(
            collective_id=0, has_side_effects=True, vmem_limit_bytes=66_000_000
        ),
    )(
        union, density_matrix, basis, weights,
        in_scale[None], in_shift[None], hidden_weight, hidden_bias[None], out_weight[None],
    )
    return density, potential


def solution(mesh):
    own = P(("space", "dev"), None)
    in_specs = (own, P(("space", "dev"), None, None), own, own, P(), P(), P(), P(), P())
    return jax.shard_map(on_device, mesh=mesh, in_specs=in_specs, out_specs=(own, own), check_vma=False)
```

time: 113 us -> 112 us (level)
  Pallas kernels: 110 us -> 108 us
    pallas_call x1, Pallas kernels: 110 us -> 108 us  [on_device(): pl.pallas_call(kernel, out_shape=(jax.ShapeDtypeStruct(weights.shape, f32...]
where the time goes in v2:
time: 112 us; the launch traced here: 111 us
  Pallas kernels  108 us (96%)
  local copies, waits for them, and re-layouts  2.92 us (3%)
    pallas_call x1, Pallas kernels, on_device(): pl.pallas_call(kernel, out_shape=(jax.ShapeDtypeStruct(weights.shape, f32...  108 us
    unnamed x2, local copies, waits for them, and re-layouts  2.92 us

profile of v2, /device:TPU:1, one launch (start us, length us, event | category | flops | bytes accessed | tf_op | source)
XLA Modules:
  0.0 111.4 jit_solution(657464062216543640)
XLA Ops:
  0.6 107.8 %shard_map.104 = (f32[2,384]{1,0:T(2,128)}, f32[16,4096]{1,0:T(8,128)}) custom-call(s32[2,8]{1,0:T(2,128)} %union_ref.1, f32[16,4096]{1,0:T(8,128)} %rows_hbm.1, f32[2,384,1024]{2,1,0:T(8,128)} %basis_hbm.1, f32[2,384]{1,0:T(2,128)} %weights_hbm.1, f32[1,256]{1,0:T(1,128)} %bitcast.4, f32[1,256]{1,0:T(1,128)} %bitcast.5, f32[256,256]{1,0:T(8,128)} %hidden_hbm.1, ...), custom_call_target="tpu_custom_call" | custom-call | tf_op jit(solution)/shard_map/pallas_call | solution.py:688
  108.5 1.2 %copy.13 = f32[2,384]{1,0:T(2,128)} copy(f32[2,384]{1,0:T(2,128)} %get-tuple-element.4) | data formatting | bytes 6144
  109.7 1.7 %copy.14 = f32[16,4096]{1,0:T(8,128)} copy(f32[16,4096]{1,0:T(8,128)} %get-tuple-element.5) | data formatting | bytes 524288
